TPU v7x, 512 devices: a whole 4x4x16 slice. The times are simulated.
512 devices in a mesh: lat: 16 (over z_hi, y, core), lon: 32 (over x, z_lo).
Axes of the slice: x: 4, y: 4, z: 16 (z_hi: 2, z_lo: 8; z = z_hi * 8 + z_lo), core: 2. Of those that a mesh axis runs over, the one named last changes fastest.
Arguments:
- bands: bfloat16 [16, 256, 320, 512], P('lat', 'lon'), may hold values from -6 to 6
- avail: int32 [16, 256, 10], P('lat', 'lon'), may hold values from 0 to 1, as said below
- latent_query: bfloat16 [4, 512], replicated, may hold values from -3 to 3
- w_band: bfloat16 [512, 1024], replicated, may hold values from -3.0935922 to 3.0935922
- w_mix: bfloat16 [512, 1536], replicated, may hold values from -3 to 3
- w_out: bfloat16 [512, 512], replicated, may hold values from -0.19921875 to 0.19921875
- offsets: int32 [5, 2], replicated, may hold values from -1 to 1, as said below
Outputs:
- encoded: bfloat16 [16, 256, 4, 512], P('lat', 'lon')
Inputs may be any that keep to these rules, and one draw needn't show every extreme that they name: `avail`: each patch has at least one available block. `offsets`: row 0 is (0, 0), rows 1 and 2 are (0, -1) and (0, 1), row 3 has latitude offset -1 and row 4 latitude offset +1; all rows differ.
All inputs are finite; a program needn't handle non-finite values.
Results may differ from a plain program's by a relative error of at most 0.03.
The roundings to bfloat16 on the way count: a program that leaves them out, or rounds other values in their place, can miss the bound.
Values may be sent and summed in bfloat16 or wider, within the bound.
No kernel may reach another device: no remote copies, remote signals or barrier semaphores. Data moves between devices by JAX's collectives and lax.ppermute only.
A program may use at most 64 MiB of HBM per device.

v0:
```python
import jax
import jax.numpy as jnp
from jax import lax
from jax.sharding import PartitionSpec as P

D = 512
HEADS = 16
HEAD = 32
BANDS = 320
BLOCK = 32
LATENTS = 4
NOFF = 5
EPS = 1e-06
NEG = -1e30


def padded(cells, sides, width):
    for axis, dim in sides:
        count = lax.axis_size(axis)
        head = lax.slice_in_dim(cells, 0, width, axis=dim)
        tail = lax.slice_in_dim(cells, cells.shape[dim] - width, cells.shape[dim], axis=dim)
        cells = jnp.concatenate(
            [
                lax.ppermute(tail, axis, [(i, (i + 1) % count) for i in range(count)]),
                cells,
                lax.ppermute(head, axis, [((i + 1) % count, i) for i in range(count)]),
            ],
            axis=dim,
        )
    return cells


def rms_rows(values):
    values = values.astype(jnp.float32)
    return values * lax.rsqrt(jnp.mean(values * values, axis=-1, keepdims=True) + EPS)


def softmax_weights(scores):
    peak_value = jnp.max(scores, axis=-1, keepdims=True)
    exponent = jnp.exp(scores - peak_value)
    return (exponent / jnp.sum(exponent, axis=-1, keepdims=True)).astype(jnp.bfloat16)


def per_device(bands, avail, latent_query, w_band, w_mix, w_out, offsets):
    columns = bands.shape[1]
    groups = HEADS // 2
    half_width = D // 2
    score_scale = HEAD ** (-0.5)
    normed = rms_rows(bands[0]).astype(jnp.bfloat16)
    key_value = jnp.dot(normed.reshape(-1, D), w_band, preferred_element_type=jnp.float32).astype(
        jnp.bfloat16
    )
    key_value = key_value.reshape(columns, BANDS, 2, HEADS, HEAD)
    queries = latent_query.reshape(LATENTS, HEADS, HEAD)
    scores = (
        jnp.einsum(
            "lhe,pbhe->plhb", queries, key_value[:, :, 0], preferred_element_type=jnp.float32
        )
        * score_scale
    )
    open_band = jnp.repeat(avail[0], BLOCK, axis=-1) > 0
    scores = jnp.where(open_band[:, None, None, :], scores, NEG)
    weights = softmax_weights(scores)
    pooled = jnp.einsum(
        "plhb,pbhe->plhe", weights, key_value[:, :, 1], preferred_element_type=jnp.float32
    )
    latent = pooled.reshape(columns, LATENTS, D) + latent_query.astype(jnp.float32)
    normal = rms_rows(latent)[None]
    mixture = jnp.dot(
        normal.astype(jnp.bfloat16).reshape(-1, D), w_mix, preferred_element_type=jnp.float32
    ).astype(jnp.bfloat16)
    mixture = mixture.reshape(1, columns, LATENTS, 3 * D)
    lat_queries = mixture[..., :D].reshape(1, columns, LATENTS, HEADS, HEAD)
    near_pairs = mixture[..., D : 2 * D]
    zonal_pairs = mixture[..., 2 * D :]
    framed = padded(near_pairs, (("lat", 0), ("lon", 1)), 1)
    zonal_row = lax.all_gather(zonal_pairs, "lon", axis=1, tiled=True)
    lat_index = lax.axis_index("lat")
    lat_count = lax.axis_size("lat")
    zero_index = jnp.zeros((), jnp.int32)
    near_keys = []
    near_open = []
    for offset_slot in range(NOFF):
        step_lat = offsets[offset_slot, 0]
        step_lon = offsets[offset_slot, 1]
        shifted = lax.dynamic_slice(
            framed, (1 + step_lat, 1 + step_lon, zero_index, zero_index), (1, columns, LATENTS, D)
        )
        near_keys.append(shifted)
        target = lat_index + step_lat
        near_open.append((target >= 0) & (target < lat_count))
    near_keys = jnp.stack(near_keys, axis=2).reshape(1, columns, NOFF * LATENTS, 2, groups, HEAD)
    open_keys = jnp.repeat(jnp.stack(near_open), LATENTS)
    scores = (
        jnp.einsum(
            "ijqhe,ijkhe->ijhqk",
            lat_queries[..., :groups, :],
            near_keys[..., 0, :, :],
            preferred_element_type=jnp.float32,
        )
        * score_scale
    )
    scores = jnp.where(open_keys, scores, NEG)
    weights = softmax_weights(scores)
    near_out = jnp.einsum(
        "ijhqk,ijkhe->ijqhe", weights, near_keys[..., 1, :, :], preferred_element_type=jnp.float32
    )
    row_keys = zonal_row.reshape(1, -1, 2, groups, HEAD)
    scores = (
        jnp.einsum(
            "ijqhe,ikhe->ijhqk",
            lat_queries[..., groups:, :],
            row_keys[:, :, 0],
            preferred_element_type=jnp.float32,
        )
        * score_scale
    )
    weights = softmax_weights(scores)
    zonal_out = jnp.einsum(
        "ijhqk,ikhe->ijqhe", weights, row_keys[:, :, 1], preferred_element_type=jnp.float32
    )
    attended = jnp.concatenate(
        [
            near_out.reshape(1, columns, LATENTS, half_width),
            zonal_out.reshape(1, columns, LATENTS, half_width),
        ],
        axis=-1,
    ).astype(jnp.bfloat16)
    update = jnp.dot(attended.reshape(-1, D), w_out, preferred_element_type=jnp.float32).reshape(
        1, columns, LATENTS, D
    )
    return (normal + update).astype(jnp.bfloat16)


def solution(mesh):
    return jax.shard_map(
        per_device,
        mesh=mesh,
        in_specs=(P("lat", "lon", None, None), P("lat", "lon", None), P(), P(), P(), P(), P()),
        out_specs=P("lat", "lon", None, None),
        check_vma=False,
    )
```

profile of v0, /device:TPU:8, one launch (start us, length us, event | category | flops | bytes accessed | tf_op | source)
XLA Modules:
  0.0 315.5 jit_solution(1022444642513698989)
XLA Ops:
  6.5 0.0 copy-start
  6.5 0.0 all-gather.2.cloned.1.call-start
  6.5 0.9 reshape.192
  7.4 0.8 add.179
  8.2 2.3 multiply_reduce_fusion
  10.5 0.0 copy-start.5
  10.6 0.1 rsqrt.24
  10.6 2.4 fusion.2
  13.0 0.0 copy-done.5
  13.0 4.7 %convolution_convert_fusion = bf16[2560,1024]{1,0:T(8,128)(2,1)} fusion(bf16[2560,512]{1,0:T(8,128)(2,1)S(1)} %fusion.2, bf16[512,1024]{1,0:T(8,128)(2,1)S(1)} %copy-done.5), kind=kOutput, calls=%fused_computation.2 | convolution fusion | flops 2686976000 | bytes 8912896 | tf_op jit(solution)/shard_map/dot_general | solution.py:50
  17.7 7.7 %copy.58 = bf16[2560,1024]{0,1:T(8,128)(2,1)} copy(bf16[2560,1024]{1,0:T(8,128)(2,1)} %convolution_convert_fusion) | data formatting | bytes 10485760 | tf_op jit(solution)/shard_map/convert_element_type | solution.py:50
  25.4 10.9 %reshape.191 = bf16[8,320,2,16,32]{1,0,4,3,2:T(8,128)(2,1)} reshape(bf16[2560,1024]{0,1:T(8,128)(2,1)} %copy.58) | data formatting | bytes 10485760 | tf_op jit(solution)/shard_map/reshape | solution.py:53
  36.2 0.0 copy-start.4
  36.2 6.5 %fusion.32 = (bf16[8,320,1,16,32]{1,0,4,3,2:T(8,128)(2,1)}, bf16[8,320,1,16,32]{1,0,4,3,2:T(8,128)(2,1)}) fusion(bf16[8,320,2,16,32]{1,0,4,3,2:T(8,128)(2,1)} %reshape.191), kind=kLoop, calls=%fused_computation.65 | loop fusion | bytes 10485760 | tf_op jit(solution)/shard_map/slice | solution.py:57
  42.7 0.0 copy-done.4
  42.8 0.1 broadcast_in_dim.24
  42.8 0.1 gt.20
  43.0 2.8 fusion.39
  45.8 0.0 copy-start.2
  45.8 3.3 %multiply_reduce_fusion.1 = (f32[8,4]{1,0:T(8,128)S(1)}, f32[8,4,16,32]{3,1,2,0:T(4,128)S(1)}) fusion(f32[4,16,32]{2,0,1:T(4,128)S(1)} %copy.64, bf16[8,320,1,16,32]{1,0,4,3,2:T(8,128)(2,1)} %get-tuple-element.6, f32[8,4,16,320]{3,1,0,2:T(4,128)S(1)} %get-tuple-element.28, f32[8,4,16]{1,0,2:T(8,128)S(1)} %get-tuple-element.27), kind=kOutput, calls=%fused_computation.41 | convolution fusion | flops 10862560 | bytes 3352704 | tf_op jit(solution)/shard_map/plhb,pbhe->plhe/dot_general | solution.py:64
  49.1 0.0 copy-start.3
  49.1 0.1 reshape.194
  49.3 0.1 rsqrt.26
  49.3 0.0 copy-done.2
  49.4 0.0 copy-done
  49.4 0.4 convolution_convert_fusion.1
  49.9 1.9 collective-permute-start
  51.8 3.6 %collective-permute-start.1 = (bf16[1,8,4,512]{3,1,2,0:T(8,128)(2,1)S(1)}, bf16[1,8,4,512]{3,1,2,0:T(8,128)(2,1)S(1)}, u32[]{:S(2)}, u32[]{:S(2)}) collective-permute-start(bf16[1,8,4,512]{3,1,2,0:T(8,128)(2,1)S(1)} %copy.87), channel_id=1, source_target_pairs={{32,0},{64,32},{96,64},{128,96},{160,128},{192,160},{224,192},{256... | collective-permute-start | bytes 98312 | tf_op jit(solution)/shard_map/ppermute | solution.py:26
  55.5 0.6 slice.101
  56.1 0.0 all-gather.2.cloned.1.call-update
  56.1 0.1 reshape.199
  56.3 0.0 collective-permute-done
  56.4 0.7 collective-permute-done.1
  57.1 3.8 %collective-permute-start.2 = (bf16[3,1,4,512]{3,1,2,0:T(2,128)(2,1)S(1)}, bf16[3,1,4,512]{3,1,2,0:T(2,128)(2,1)S(1)}, u32[]{:S(2)}, u32[]{:S(2)}) collective-permute-start(bf16[3,1,4,512]{3,1,2,0:T(2,128)(2,1)S(1)} %get-tuple-element.13), channel_id=1, source_target_pairs={{0,1},{1,2},{2,3},{3,4},{4,5},{5,6},{6,7},{7,8},{8,9},{9,10},{10,1... | collective-permute-start | bytes 36872 | tf_op jit(solution)/shard_map/ppermute | solution.py:24
  60.9 13.6 %collective-permute-start.3 = (bf16[3,1,4,512]{3,1,2,0:T(2,128)(2,1)S(1)}, bf16[3,1,4,512]{3,1,2,0:T(2,128)(2,1)S(1)}, u32[]{:S(2)}, u32[]{:S(2)}) collective-permute-start(bf16[3,1,4,512]{3,1,2,0:T(2,128)(2,1)S(1)} %get-tuple-element.14), channel_id=1, source_target_pairs={{1,0},{2,1},{3,2},{4,3},{5,4},{6,5},{7,6},{8,7},{9,8},{10,9},{11,1... | collective-permute-start | bytes 36872 | tf_op jit(solution)/shard_map/ppermute | solution.py:26
  74.6 0.0 copy-done.3
  74.6 0.7 fusion.38
  90.9 0.1 copy.65
  91.0 0.1 stack.47
  91.1 0.1 broadcast_in_dim.40
  91.2 0.1 reshape.198
  91.3 0.1 reshape.193
  91.5 0.0 collective-permute-done.2
  91.5 0.0 collective-permute-done.3
  91.5 0.1 pad_maximum_fusion
  91.8 0.3 reshape.196
  92.1 0.2 fusion.34
  92.3 0.5 fusion.41
  92.8 0.3 fusion.16
  93.2 0.1 concatenate.20
  93.3 197.7 %all-gather.2.cloned.1.call-done = bf16[1,256,4,512]{3,2,0,1:T(4,128)(2,1)} async-done(((bf16[1,8,4,512]{3,2,0,1:T(4,128)(2,1)}), bf16[1,256,4,512]{3,2,0,1:T(4,128)(2,1)}) %all-gather.2.cloned.1.call-update) | async-done | bytes 1048592 | tf_op jit(solution)/shard_map/all_gather | solution.py:77
  291.0 6.0 %reshape.202 = bf16[1,1024,2,8,32]{4,3,2,1,0:T(8,128)(2,1)} reshape(bf16[1,256,4,512]{3,2,0,1:T(4,128)(2,1)} %all-gather.2.cloned.1.call-done) | data formatting | bytes 2097152 | tf_op jit(solution)/shard_map/reshape | solution.py:108
  297.0 4.5 %fusion.33 = (bf16[1,1024,1,8,32]{4,3,2,1,0:T(8,128)(2,1)}, bf16[1,1024,1,8,32]{4,3,2,1,0:T(8,128)(2,1)}) fusion(bf16[1,1024,2,8,32]{4,3,2,1,0:T(8,128)(2,1)} %reshape.202), kind=kLoop, calls=%fused_computation.66 | loop fusion | bytes 2097152 | tf_op jit(solution)/shard_map/slice | solution.py:113
  301.5 2.5 copy.93
  304.0 2.5 copy.92
  306.4 0.4 fusion.40
  306.8 0.0 copy-start.1
  306.8 0.3 fusion.19
  307.1 0.4 fusion.15
  307.5 0.1 concatenate.21
  307.6 0.2 copy-done.1
  307.9 0.2 fusion.18
  308.1 0.6 copy.79
  (25 shorter events, 0.5 us)
Async XLA Ops:
  6.5 42.8 %copy-start = (bf16[512,1536]{1,0:T(8,128)(2,1)S(1)}, bf16[512,1536]{1,0:T(8,128)(2,1)}, u32[]{:S(2)}) copy-start(bf16[512,1536]{1,0:T(8,128)(2,1)} %param.11) | copy-start | bytes 4718596
  6.5 284.5 %all-gather.2.cloned.1.call-start = ((), (), s32[]{:S(2)}) async-start(), calls=%async_computation | async-start | bytes 1081344 | tf_op jit(solution)/shard_map/all_gather | solution.py:77
  10.5 2.5 copy-start.5
  36.2 6.5 %copy-start.4 = (s32[1,8,10]{2,1,0:T(8,128)S(1)}, s32[1,8,10]{2,1,0:T(8,128)}, u32[]{:S(2)}) copy-start(s32[1,8,10]{2,1,0:T(8,128)} %param.8) | copy-start | bytes 964
  45.8 3.5 %copy-start.2 = (bf16[4,512]{1,0:T(4,128)(2,1)S(1)}, bf16[4,512]{1,0:T(4,128)(2,1)}, u32[]{:S(2)}) copy-start(bf16[4,512]{1,0:T(4,128)(2,1)} %param.9) | copy-start | bytes 12292
  49.1 25.5 %copy-start.3 = (s32[5,2]{0,1:T(2,128)S(1)}, s32[5,2]{0,1:T(2,128)}, u32[]{:S(2)}) copy-start(s32[5,2]{0,1:T(2,128)} %param.13) | copy-start | bytes 124
  49.9 6.4 %collective-permute-start = (bf16[1,8,4,512]{3,1,2,0:T(8,128)(2,1)S(1)}, bf16[1,8,4,512]{3,1,2,0:T(8,128)(2,1)S(1)}, u32[]{:S(2)}, u32[]{:S(2)}) collective-permute-start(bf16[1,8,4,512]{3,1,2,0:T(8,128)(2,1)S(1)} %copy.87), channel_id=1, source_target_pairs={{0,32},{32,64},{64,96},{96,128},{128,160},{160,192},{192,224},{224... | collective-permute-start | bytes 98312 | tf_op jit(solution)/shard_map/ppermute | solution.py:24
  51.8 5.2 %collective-permute-start.1 = (bf16[1,8,4,512]{3,1,2,0:T(8,128)(2,1)S(1)}, bf16[1,8,4,512]{3,1,2,0:T(8,128)(2,1)S(1)}, u32[]{:S(2)}, u32[]{:S(2)}) collective-permute-start(bf16[1,8,4,512]{3,1,2,0:T(8,128)(2,1)S(1)} %copy.87), channel_id=1, source_target_pairs={{32,0},{64,32},{96,64},{128,96},{160,128},{192,160},{224,192},{256... | collective-permute-start | bytes 98312 | tf_op jit(solution)/shard_map/ppermute | solution.py:26
  57.1 34.4 %collective-permute-start.2 = (bf16[3,1,4,512]{3,1,2,0:T(2,128)(2,1)S(1)}, bf16[3,1,4,512]{3,1,2,0:T(2,128)(2,1)S(1)}, u32[]{:S(2)}, u32[]{:S(2)}) collective-permute-start(bf16[3,1,4,512]{3,1,2,0:T(2,128)(2,1)S(1)} %get-tuple-element.13), channel_id=1, source_target_pairs={{0,1},{1,2},{2,3},{3,4},{4,5},{5,6},{6,7},{7,8},{8,9},{9,10},{10,1... | collective-permute-start | bytes 36872 | tf_op jit(solution)/shard_map/ppermute | solution.py:24
  60.9 30.6 %collective-permute-start.3 = (bf16[3,1,4,512]{3,1,2,0:T(2,128)(2,1)S(1)}, bf16[3,1,4,512]{3,1,2,0:T(2,128)(2,1)S(1)}, u32[]{:S(2)}, u32[]{:S(2)}) collective-permute-start(bf16[3,1,4,512]{3,1,2,0:T(2,128)(2,1)S(1)} %get-tuple-element.14), channel_id=1, source_target_pairs={{1,0},{2,1},{3,2},{4,3},{5,4},{6,5},{7,6},{8,7},{9,8},{10,9},{11,1... | collective-permute-start | bytes 36872 | tf_op jit(solution)/shard_map/ppermute | solution.py:26
  306.8 1.0 copy-start.1
Sparse Core Ops, SparseCore 0:
  56.2 234.7 all-gather.1
where the time goes:
time: 317 us; the launch traced here: 316 us
  waiting for transfers between devices  198 us (62%)
  local copies, waits for them, and re-layouts  46.6 us (15%)
  between operations  29.4 us (9%)
  starting transfers between devices  23 us (7%)
  matrix products  13 us (4%)
  other arithmetic  5.12 us (2%)
    all_gather x1, waiting for transfers between devices, per_device(): zonal_row = lax.all_gather(zonal_pairs, 'lon', axis=1, tiled=True)  198 us
    ppermute x2, starting transfers between devices, padded(): lax.ppermute(head, axis, [((i + 1) % count, i) for i in range(count)])  17.3 us
    reshape x1, local copies, waits for them, and re-layouts, per_device(): key_value = key_value.reshape(columns, BANDS, 2, HEADS, HEAD)  10.9 us
    convert_element_type x1, local copies, waits for them, and re-layouts, per_device(): jnp.dot(normed.reshape(-1, D), w_band, preferred_element_type=jnp.float32)  7.68 us
    slice x1, local copies, waits for them, and re-layouts, per_device(): key_value[:, :, 0]  6.54 us
  transfers between devices with their start and end apart: 5, of which 2 were waited for; matrix products, arithmetic and copies ran while one was open for 1% of the time, Pallas kernels for 0%

commit v1 on v0

--- a/solution.py
+++ b/solution.py
@@ -74,7 +74,9 @@
     near_pairs = mixture[..., D : 2 * D]
     zonal_pairs = mixture[..., 2 * D :]
     framed = padded(near_pairs, (("lat", 0), ("lon", 1)), 1)
-    zonal_row = lax.all_gather(zonal_pairs, "lon", axis=1, tiled=True)
+    zonal_row = jnp.concatenate(
+        lax.all_to_all(jnp.stack([zonal_pairs] * lax.axis_size("lon")), "lon", 0, 0), axis=1
+    )
     lat_index = lax.axis_index("lat")
     lat_count = lax.axis_size("lat")
     zero_index = jnp.zeros((), jnp.int32)

time: 317 us -> 160 us (0.50)
  the two profiles are of different devices: /device:TPU:8 before, /device:TPU:66 now
where the time goes in v1:
time: 160 us; the launch traced here: 159 us
  local copies, waits for them, and re-layouts  49.8 us (31%)
  starting transfers between devices  37.2 us (23%)
  waiting for transfers between devices  36.3 us (23%)
  between operations  15.9 us (10%)
  matrix products  14.9 us (9%)
  other arithmetic  5.16 us (3%)
    ppermute x2, waiting for transfers between devices, padded(): lax.ppermute(tail, axis, [(i, (i + 1) % count) for i in range(count)])  36.3 us
    ppermute x2, starting transfers between devices, padded(): lax.ppermute(head, axis, [((i + 1) % count, i) for i in range(count)])  18.6 us
    all_to_all x1, starting transfers between devices, per_device(): lax.all_to_all(jnp.stack([zonal_pairs] * lax.axis_size('lon')), 'lon', 0, 0)  14.8 us
    reshape x1, local copies, waits for them, and re-layouts, per_device(): key_value = key_value.reshape(columns, BANDS, 2, HEADS, HEAD)  10.9 us
    unnamed x19, local copies, waits for them, and re-layouts  7.71 us
    convert_element_type x1, local copies, waits for them, and re-layouts, per_device(): jnp.dot(normed.reshape(-1, D), w_band, preferred_element_type=jnp.float32)  7.68 us
    slice x1, local copies, waits for them, and re-layouts, per_device(): key_value[:, :, 0]  6.54 us
    dot_general x1, matrix products, per_device(): jnp.dot(normed.reshape(-1, D), w_band, preferred_element_type=jnp.float32)  4.66 us
  transfers between devices with their start and end apart: 5, of which 1 were waited for; matrix products, arithmetic and copies ran while one was open for 6% of the time, Pallas kernels for 0%

profile of v1, /device:TPU:66, one launch (start us, length us, event | category | flops | bytes accessed | tf_op | source)
XLA Modules:
  0.0 159.2 jit_solution(5573635578674334126)
XLA Ops:
  0.0 0.0 copy-start
  0.0 0.9 reshape.192
  0.9 0.8 add.179
  1.7 2.3 %multiply_reduce_fusion = f32[8,320]{1,0:T(8,128)S(1)} fusion(bf16[1,8,320,512]{3,2,1,0:T(8,128)(2,1)} %param.7), kind=kLoop, calls=%fused_computation.5 | loop fusion | flops 3929600 | bytes 2631680 | tf_op jit(solution)/shard_map/reduce_sum | solution.py:35
  4.0 0.0 copy-start.5
  4.0 0.1 rsqrt.24
  4.1 2.4 %fusion.2 = bf16[2560,512]{1,0:T(8,128)(2,1)S(1)} fusion(f32[2560]{0:T(1024)S(1)} %rsqrt.24, bf16[1,8,320,512]{3,2,1,0:T(8,128)(2,1)} %param.7), kind=kLoop, calls=%fused_computation.4 | loop fusion | flops 3932160 | bytes 5253120 | tf_op jit(solution)/shard_map/convert_element_type | solution.py:49
  6.5 0.0 copy-done.5
  6.5 4.7 %convolution_convert_fusion = bf16[2560,1024]{1,0:T(8,128)(2,1)} fusion(bf16[2560,512]{1,0:T(8,128)(2,1)S(1)} %fusion.2, bf16[512,1024]{1,0:T(8,128)(2,1)S(1)} %copy-done.5), kind=kOutput, calls=%fused_computation.2 | convolution fusion | flops 2686976000 | bytes 8912896 | tf_op jit(solution)/shard_map/dot_general | solution.py:50
  11.1 7.7 %copy.42 = bf16[2560,1024]{0,1:T(8,128)(2,1)} copy(bf16[2560,1024]{1,0:T(8,128)(2,1)} %convolution_convert_fusion) | data formatting | bytes 10485760 | tf_op jit(solution)/shard_map/convert_element_type | solution.py:50
  18.8 10.9 %reshape.191 = bf16[8,320,2,16,32]{1,0,4,3,2:T(8,128)(2,1)} reshape(bf16[2560,1024]{0,1:T(8,128)(2,1)} %copy.42) | data formatting | bytes 10485760 | tf_op jit(solution)/shard_map/reshape | solution.py:53
  29.7 6.5 %fusion.32 = (bf16[8,320,1,16,32]{1,0,4,3,2:T(8,128)(2,1)}, bf16[8,320,1,16,32]{1,0,4,3,2:T(8,128)(2,1)}) fusion(bf16[8,320,2,16,32]{1,0,4,3,2:T(8,128)(2,1)} %reshape.191), kind=kLoop, calls=%fused_computation.71 | loop fusion | bytes 10485760 | tf_op jit(solution)/shard_map/slice | solution.py:57
  36.2 0.0 copy-done.4
  36.2 0.1 broadcast_in_dim.24
  36.3 0.1 gt.20
  36.4 2.8 %fusion.38 = (f32[8,4,16]{1,0,2:T(8,128)S(1)}, f32[8,4,16,320]{3,1,0,2:T(4,128)S(1)}) fusion(bf16[8,320,1,16,32]{1,0,4,3,2:T(8,128)(2,1)} %get-tuple-element.5, pred[8,320]{1,0:T(8,128)(4,1)S(1)} %gt.20, bf16[4,16,32,1]{2,1,0,3:T(8,128)(2,1)S(1)} %bitcast.144), kind=kOutput, calls=%fused_computation.77 | convolution fusion | flops 11141439 | bytes 3285504 | tf_op jit(solution)/shard_map/sub | solution.py:40
  39.3 3.2 %multiply_reduce_fusion.1 = (f32[8,4]{1,0:T(8,128)S(1)}, f32[8,4,16,32]{3,1,2,0:T(4,128)S(1)}) fusion(f32[4,16,32]{2,0,1:T(4,128)S(1)} %copy.48, bf16[8,320,1,16,32]{1,0,4,3,2:T(8,128)(2,1)} %get-tuple-element.6, f32[8,4,16,320]{3,1,0,2:T(4,128)S(1)} %get-tuple-element.34, f32[8,4,16]{1,0,2:T(8,128)S(1)} %get-tuple-element.33), kind=kOutput, calls=%fused_computation.41 | convolution fusion | flops 10862560 | bytes 3352704 | tf_op jit(solution)/shard_map/plhb,pbhe->plhe/dot_general | solution.py:64
  42.6 0.1 reshape.194
  42.7 0.1 rsqrt.26
  42.8 0.0 copy-done.2
  42.8 0.0 copy-done
  42.9 0.4 convolution_convert_fusion.1
  43.4 1.5 stack.38
  44.8 14.8 %all-to-all-start = ((bf16[32,1,8,4,512]{4,3,2,1,0:T(4,128)(2,1)}), bf16[32,1,8,4,512]{4,3,2,1,0:T(4,128)(2,1)S(1)}, u32[]{:S(2)}, u32[]{:S(2)}) async-start(bf16[32,1,8,4,512]{4,3,2,1,0:T(4,128)(2,1)} %stack.38), calls=%async_computation | async-start | bytes 2097152 | tf_op jit(solution)/shard_map/all_to_all | solution.py:78
  59.6 1.9 %collective-permute-start = (bf16[1,8,4,512]{3,2,1,0:T(4,128)(2,1)S(1)}, bf16[1,8,4,512]{3,2,1,0:T(4,128)(2,1)S(1)}, u32[]{:S(2)}, u32[]{:S(2)}) collective-permute-start(bf16[1,8,4,512]{3,2,1,0:T(4,128)(2,1)S(1)} %get-tuple-element.20), channel_id=1, source_target_pairs={{0,32},{32,64},{64,96},{96,128},{128,160},{160,192},{192,224},{224... | collective-permute-start | bytes 98312 | tf_op jit(solution)/shard_map/ppermute | solution.py:24
  61.5 14.5 %collective-permute-start.1 = (bf16[1,8,4,512]{3,2,1,0:T(4,128)(2,1)S(1)}, bf16[1,8,4,512]{3,2,1,0:T(4,128)(2,1)S(1)}, u32[]{:S(2)}, u32[]{:S(2)}) collective-permute-start(bf16[1,8,4,512]{3,2,1,0:T(4,128)(2,1)S(1)} %get-tuple-element.20), channel_id=1, source_target_pairs={{32,0},{64,32},{96,64},{128,96},{160,128},{192,160},{224,192},{256... | collective-permute-start | bytes 98312 | tf_op jit(solution)/shard_map/ppermute | solution.py:26
  76.0 0.1 reshape.199
  76.2 36.3 %collective-permute-done = bf16[1,8,4,512]{3,2,1,0:T(4,128)(2,1)S(1)} collective-permute-done((bf16[1,8,4,512]{3,2,1,0:T(4,128)(2,1)S(1)}, bf16[1,8,4,512]{3,2,1,0:T(4,128)(2,1)S(1)}, u32[]{:S(2)}, u32[]{:S(2)}) %collective-permute-start) | collective-permute-done | bytes 32800 | tf_op jit(solution)/shard_map/ppermute | solution.py:24
  112.5 0.0 collective-permute-done.1
  112.5 1.9 %collective-permute-start.2 = (bf16[3,1,4,512]{3,2,1,0:T(4,128)(2,1)S(1)}, bf16[3,1,4,512]{3,2,1,0:T(4,128)(2,1)S(1)}, u32[]{:S(2)}, u32[]{:S(2)}) collective-permute-start(bf16[3,1,4,512]{3,2,1,0:T(4,128)(2,1)S(1)} %get-tuple-element.18), channel_id=1, source_target_pairs={{0,1},{1,2},{2,3},{3,4},{4,5},{5,6},{6,7},{7,8},{8,9},{9,10},{10,1... | collective-permute-start | bytes 36872 | tf_op jit(solution)/shard_map/ppermute | solution.py:24
  114.5 4.1 %collective-permute-start.3 = (bf16[3,1,4,512]{3,2,1,0:T(4,128)(2,1)S(1)}, bf16[3,1,4,512]{3,2,1,0:T(4,128)(2,1)S(1)}, u32[]{:S(2)}, u32[]{:S(2)}) collective-permute-start(bf16[3,1,4,512]{3,2,1,0:T(4,128)(2,1)S(1)} %get-tuple-element.19), channel_id=1, source_target_pairs={{1,0},{2,1},{3,2},{4,3},{5,4},{6,5},{7,6},{8,7},{9,8},{10,9},{11,1... | collective-permute-start | bytes 36872 | tf_op jit(solution)/shard_map/ppermute | solution.py:26
  118.6 0.0 copy-done.3
  118.6 0.7 fusion.37
  134.8 0.1 copy.49
  134.9 0.1 stack.37
  135.0 0.1 broadcast_in_dim.40
  135.1 0.1 reshape.198
  135.1 0.1 reshape.193
  135.4 0.0 collective-permute-done.2
  135.4 0.0 collective-permute-done.3
  135.4 0.1 pad_maximum_fusion
  135.5 0.1 constant_dynamic-slice_fusion
  135.6 0.6 bitcast_dynamic-update-slice_fusion.4
  136.2 0.6 bitcast_dynamic-update-slice_fusion.3
  136.8 0.6 bitcast_dynamic-update-slice_fusion.2
  137.5 0.6 bitcast_dynamic-update-slice_fusion.1
  138.1 0.6 bitcast_dynamic-update-slice_fusion
  138.7 1.3 reshape.196
  140.0 1.0 fusion.34
  141.1 1.5 fusion.40
  142.5 1.3 fusion.16
  143.9 0.1 concatenate.20
  144.0 0.0 all-to-all-done
  144.0 3.6 %reshape_reshape.3 = bf16[1,1024,2,8,32]{4,3,2,1,0:T(8,128)(2,1)} reshape(bf16[32,1,8,4,512]{4,3,2,1,0:T(4,128)(2,1)S(1)} %all-to-all-done) | data formatting | bytes 2097152 | tf_op jit(solution)/shard_map/reshape;reshape | solution.py:110
  147.6 4.5 %fusion.33 = (bf16[1,1024,1,8,32]{4,3,2,1,0:T(8,128)(2,1)}, bf16[1,1024,1,8,32]{4,3,2,1,0:T(8,128)(2,1)}) fusion(bf16[1,1024,2,8,32]{4,3,2,1,0:T(8,128)(2,1)} %reshape_reshape.3), kind=kLoop, calls=%fused_computation.72 | loop fusion | bytes 2097152 | tf_op jit(solution)/shard_map/slice | solution.py:115
  152.0 2.5 %copy.79 = bf16[1,1024,1,8,32]{1,4,3,2,0:T(8,128)(2,1)S(1)} copy(bf16[1,1024,1,8,32]{4,3,2,1,0:T(8,128)(2,1)} %get-tuple-element.7) | data formatting | bytes 1048576
  154.5 2.5 %copy.78 = bf16[1,1024,1,8,32]{1,4,3,2,0:T(8,128)(2,1)S(1)} copy(bf16[1,1024,1,8,32]{4,3,2,1,0:T(8,128)(2,1)} %get-tuple-element.8) | data formatting | bytes 1048576
  157.0 0.4 fusion.39
  157.4 0.3 fusion.19
  157.7 0.4 fusion.15
  158.1 0.1 concatenate.21
  158.2 0.2 copy-done.1
  158.4 0.2 fusion.18
  158.6 0.6 copy.66
  (20 shorter events, 0.3 us)
Async XLA Ops:
  0.0 42.9 %copy-start = (bf16[512,1536]{1,0:T(8,128)(2,1)S(1)}, bf16[512,1536]{1,0:T(8,128)(2,1)}, u32[]{:S(2)}) copy-start(bf16[512,1536]{1,0:T(8,128)(2,1)} %param.11) | copy-start | bytes 4718596
  4.0 2.5 %copy-start.5 = (bf16[512,1024]{1,0:T(8,128)(2,1)S(1)}, bf16[512,1024]{1,0:T(8,128)(2,1)}, u32[]{:S(2)}) copy-start(bf16[512,1024]{1,0:T(8,128)(2,1)} %param.10) | copy-start | bytes 3145732
  29.7 6.5 %copy-start.4 = (s32[1,8,10]{2,1,0:T(8,128)S(1)}, s32[1,8,10]{2,1,0:T(8,128)}, u32[]{:S(2)}) copy-start(s32[1,8,10]{2,1,0:T(8,128)} %param.8) | copy-start | bytes 964
  39.3 3.5 %copy-start.2 = (bf16[4,512]{1,0:T(4,128)(2,1)S(1)}, bf16[4,512]{1,0:T(4,128)(2,1)}, u32[]{:S(2)}) copy-start(bf16[4,512]{1,0:T(4,128)(2,1)} %param.9) | copy-start | bytes 12292
  42.7 75.9 %copy-start.3 = (s32[5,2]{0,1:T(2,128)S(1)}, s32[5,2]{0,1:T(2,128)}, u32[]{:S(2)}) copy-start(s32[5,2]{0,1:T(2,128)} %param.13) | copy-start | bytes 124
  44.8 99.2 %all-to-all-start = ((bf16[32,1,8,4,512]{4,3,2,1,0:T(4,128)(2,1)}), bf16[32,1,8,4,512]{4,3,2,1,0:T(4,128)(2,1)S(1)}, u32[]{:S(2)}, u32[]{:S(2)}) async-start(bf16[32,1,8,4,512]{4,3,2,1,0:T(4,128)(2,1)} %stack.38), calls=%async_computation | async-start | bytes 2097152 | tf_op jit(solution)/shard_map/all_to_all | solution.py:78
  59.6 52.9 %collective-permute-start = (bf16[1,8,4,512]{3,2,1,0:T(4,128)(2,1)S(1)}, bf16[1,8,4,512]{3,2,1,0:T(4,128)(2,1)S(1)}, u32[]{:S(2)}, u32[]{:S(2)}) collective-permute-start(bf16[1,8,4,512]{3,2,1,0:T(4,128)(2,1)S(1)} %get-tuple-element.20), channel_id=1, source_target_pairs={{0,32},{32,64},{64,96},{96,128},{128,160},{160,192},{192,224},{224... | collective-permute-start | bytes 98312 | tf_op jit(solution)/shard_map/ppermute | solution.py:24
  61.5 51.0 %collective-permute-start.1 = (bf16[1,8,4,512]{3,2,1,0:T(4,128)(2,1)S(1)}, bf16[1,8,4,512]{3,2,1,0:T(4,128)(2,1)S(1)}, u32[]{:S(2)}, u32[]{:S(2)}) collective-permute-start(bf16[1,8,4,512]{3,2,1,0:T(4,128)(2,1)S(1)} %get-tuple-element.20), channel_id=1, source_target_pairs={{32,0},{64,32},{96,64},{128,96},{160,128},{192,160},{224,192},{256... | collective-permute-start | bytes 98312 | tf_op jit(solution)/shard_map/ppermute | solution.py:26
  112.5 22.8 %collective-permute-start.2 = (bf16[3,1,4,512]{3,2,1,0:T(4,128)(2,1)S(1)}, bf16[3,1,4,512]{3,2,1,0:T(4,128)(2,1)S(1)}, u32[]{:S(2)}, u32[]{:S(2)}) collective-permute-start(bf16[3,1,4,512]{3,2,1,0:T(4,128)(2,1)S(1)} %get-tuple-element.18), channel_id=1, source_target_pairs={{0,1},{1,2},{2,3},{3,4},{4,5},{5,6},{6,7},{7,8},{8,9},{9,10},{10,1... | collective-permute-start | bytes 36872 | tf_op jit(solution)/shard_map/ppermute | solution.py:24
  114.5 20.9 %collective-permute-start.3 = (bf16[3,1,4,512]{3,2,1,0:T(4,128)(2,1)S(1)}, bf16[3,1,4,512]{3,2,1,0:T(4,128)(2,1)S(1)}, u32[]{:S(2)}, u32[]{:S(2)}) collective-permute-start(bf16[3,1,4,512]{3,2,1,0:T(4,128)(2,1)S(1)} %get-tuple-element.19), channel_id=1, source_target_pairs={{1,0},{2,1},{3,2},{4,3},{5,4},{6,5},{7,6},{8,7},{9,8},{10,9},{11,1... | collective-permute-start | bytes 36872 | tf_op jit(solution)/shard_map/ppermute | solution.py:26
  157.3 1.0 copy-start.1
